TPU v7x, 512 devices: a whole 4x8x8 slice. The times are simulated.
512 devices in a mesh: dp: 32 (over x, z), tp: 16 (over y, core).
Axes of the slice: x: 4, y: 8, z: 8, core: 2. Of those that a mesh axis runs over, the one named last changes fastest.
Arguments:
- queries: bfloat16 [1024, 128, 576], P(('dp', 'tp')), may hold values from -40 to 40
- latent_cache: bfloat16 [1024, 256, 576], P(('dp', 'tp')), may hold values from -5 to 5
- lengths: int32 [1024], P(('dp', 'tp')), may hold values from 1 to 256, 65536 in all
- value_weight: bfloat16 [128, 512, 128], P('tp'), may hold values from -0.25 to 0.25
- output_weight: bfloat16 [16384, 7168], P('tp', 'dp'), may hold values from -0.046875 to 0.046875
Outputs:
- attended: bfloat16 [1024, 7168], P(('dp', 'tp'))
All inputs are finite; a program needn't handle non-finite values. No bound on the sum of `lengths` on one device may be relied on, other than what follows from the above.
Results may differ from a plain program's by a relative error of at most 0.0065.
Values may be sent and summed in bfloat16 or wider, within the bound.
No kernel may reach another device: no remote copies, remote signals or barrier semaphores. Data moves between devices by JAX's collectives and lax.ppermute only.
A program may use at most 64 MiB of HBM per device.

v0:
```python
import jax
import jax.numpy as jnp
from jax import lax
from jax.sharding import PartitionSpec as P

score_scale = 192.0 ** (-0.5)


def local(queries, latent_cache, lengths, value_weight, output_weight):
    requests = queries.shape[0]
    groups = lax.axis_size("tp")
    columns = lax.axis_size("dp")
    latent_width = value_weight.shape[1]
    scores = (
        jnp.einsum("rhe,rje->rhj", queries, latent_cache, preferred_element_type=jnp.float32)
        * score_scale
    )
    alive_mask = lax.broadcasted_iota(jnp.int32, scores.shape, 2) < lengths[:, None, None]
    scores = jnp.where(alive_mask, scores, -1e30)
    row_max = jnp.max(scores, axis=2, keepdims=True)
    powers = jnp.exp(scores - row_max)
    weights = (powers / jnp.sum(powers, axis=2, keepdims=True)).astype(jnp.bfloat16)
    mixture = jnp.einsum("rhj,rje->rhe", weights, latent_cache, preferred_element_type=jnp.float32)
    latent = mixture[:, :, :latent_width].astype(jnp.bfloat16)
    swapped = lax.all_to_all(latent, "tp", split_axis=1, concat_axis=0, tiled=True)
    values = jnp.einsum("qhd,hde->qhe", swapped, value_weight, preferred_element_type=jnp.float32)
    values = values.astype(jnp.bfloat16).reshape(groups, requests, -1)
    everyone = lax.all_gather(values, "dp", axis=1, tiled=True)
    all_values = everyone.reshape(groups * columns * requests, -1)
    summed = lax.psum_scatter(
        jnp.dot(all_values, output_weight, preferred_element_type=jnp.float32),
        "tp",
        scatter_dimension=0,
        tiled=True,
    )
    rounded = summed.astype(jnp.bfloat16)
    return lax.all_to_all(rounded, "dp", split_axis=0, concat_axis=1, tiled=True)


def solution(mesh):
    return jax.shard_map(
        local,
        mesh=mesh,
        in_specs=(
            P(("dp", "tp"), None, None),
            P(("dp", "tp"), None, None),
            P(("dp", "tp")),
            P("tp", None, None),
            P("tp", "dp"),
        ),
        out_specs=P(("dp", "tp"), None),
        check_vma=False,
    )
```

profile of v0, /device:TPU:2, one launch (start us, length us, event | category | flops | bytes accessed | tf_op | source)
XLA Modules:
  0.0 203.4 jit_solution(8184634764328297941)
XLA Ops:
  6.5 0.0 copy-start
  6.5 0.0 all-gather.2.cloned.1.call-start
  6.5 1.5 fusion.3
  8.1 0.2 fusion.8
  8.3 1.6 fusion.5
  9.9 0.3 copy.16
  10.2 18.2 %all_to_all.37 = bf16[2,128,512]{2,0,1:T(2,128)(2,1)S(1)} all-to-all(bf16[2,128,512]{2,0,1:T(2,128)(2,1)S(1)} %copy.16), channel_id=1, replica_groups=mesh['dp'=32,'tp'=16] {'tp'}, dimensions={1} | all-to-all | bytes 524288 | tf_op jit(solution)/shard_map/all_to_all | solution.py:25
  28.4 0.2 copy.23
  28.6 0.1 all_to_all.30
  28.7 0.0 copy-done
  28.7 0.3 fusion.4
  29.0 0.6 copy.19
  29.7 0.0 all-gather.2.cloned.1.call-update
  29.7 0.0 copy-start.1
  29.7 0.0 reduce-scatter.2.cloned.1.call-start
  29.7 83.9 %all-gather.2.cloned.1.call-done = bf16[16,64,1024]{2,0,1:T(8,128)(2,1)} async-done(((bf16[16,2,1024]{2,0,1:T(8,128)(2,1)}), bf16[16,64,1024]{2,0,1:T(8,128)(2,1)}) %all-gather.2.cloned.1.call-update) | async-done | bytes 2097168 | tf_op jit(solution)/shard_map/all_gather | solution.py:28
  113.6 2.7 %copy.20 = bf16[16,64,1024]{2,1,0:T(8,128)(2,1)S(1)} copy(bf16[16,64,1024]{2,0,1:T(8,128)(2,1)} %all-gather.2.cloned.1.call-done) | data formatting | bytes 4194304 | tf_op jit(solution)/shard_map/all_gather | solution.py:28
  116.4 0.0 copy-done.1
  116.4 1.7 fusion.9
  118.1 0.0 reduce-scatter.2.cloned.1.call-update
  118.2 57.8 %reduce-scatter.2.cloned.1.call-done = f32[64,224]{1,0:T(8,128)} async-done(((f32[1024,224]{1,0:T(8,128)}), f32[64,224]{1,0:T(8,128)}) %reduce-scatter.2.cloned.1.call-update) | async-done | bytes 57360 | tf_op jit(solution)/shard_map/reduce_scatter | solution.py:30
  175.9 0.8 convert_element_type.16
  176.8 19.0 %all_to_all.38 = bf16[32,2,224]{2,1,0:T(2,128)(2,1)S(1)} all-to-all(bf16[32,2,224]{2,1,0:T(2,128)(2,1)S(1)} %all_to_all.31), channel_id=1, replica_groups=mesh['dp'=32,'tp'=16] {'dp'}, dimensions={0} | all-to-all | bytes 57344 | tf_op jit(solution)/shard_map/all_to_all | solution.py:37
  195.8 0.7 all_to_all.34
  (5 shorter events, 0.1 us)
Async XLA Ops:
  6.5 22.1 %copy-start = (bf16[8,512,128]{2,1,0:T(8,128)(2,1)S(1)}, bf16[8,512,128]{2,1,0:T(8,128)(2,1)}, u32[]{:S(2)}) copy-start(bf16[8,512,128]{2,1,0:T(8,128)(2,1)} %param.8) | copy-start | bytes 3145732
  6.5 107.1 %all-gather.2.cloned.1.call-start = ((), (), s32[]{:S(2)}) async-start(), calls=%async_computation.3 | async-start | bytes 2162688 | tf_op jit(solution)/shard_map/all_gather | solution.py:28
  29.7 86.7 %copy-start.1 = (bf16[1024,224]{0,1:T(8,128)(2,1)S(1)}, bf16[1024,224]{0,1:T(8,128)(2,1)}, u32[]{:S(2)}) copy-start(bf16[1024,224]{0,1:T(8,128)(2,1)} %param.9) | copy-start | bytes 1376260
  29.7 146.2 %reduce-scatter.2.cloned.1.call-start = ((), (), s32[]{:S(2)}) async-start(), calls=%async_computation.4 | async-start | bytes 1114112 | tf_op jit(solution)/shard_map/reduce_scatter | solution.py:30
Sparse Core Ops, SparseCore 0:
  29.8 83.7 all-gather.1
  118.3 57.6 reduce-scatter.1
where the time goes:
time: 204 us; the launch traced here: 203 us
  waiting for transfers between devices  142 us (70%)
  blocking collectives  37.2 us (18%)
  between operations  13.5 us (7%)
  matrix products  5.14 us (3%)
  local copies, waits for them, and re-layouts  4.78 us (2%)
    all_gather x1, waiting for transfers between devices, local(): everyone = lax.all_gather(values, 'dp', axis=1, tiled=True)  83.9 us
    reduce_scatter x1, waiting for transfers between devices, local(): lax.psum_scatter(jnp.dot(all_values, output_weight, preferred_element_typ...  57.8 us
    all_to_all x1, blocking collectives, local(): lax.all_to_all(rounded, 'dp', split_axis=0, concat_axis=1, tiled=True)  19 us
    all_to_all x1, blocking collectives, local(): lax.all_to_all(latent, 'tp', split_axis=1, concat_axis=0, tiled=True)  18.2 us
  transfers between devices with their start and end apart: 2, of which 2 were waited for; matrix products, arithmetic and copies ran while one was open for 0% of the time, Pallas kernels for 0%

commit v1 on v0

--- a/solution.py
+++ b/solution.py
@@ -4,6 +4,12 @@
 from jax.sharding import PartitionSpec as P
 
 score_scale = 192.0 ** (-0.5)
+
+
+def gather_from_all(x, axis, dim):
+    devices = lax.axis_size(axis)
+    repeats = [devices if d == dim else 1 for d in range(x.ndim)]
+    return lax.all_to_all(jnp.tile(x, repeats), axis, split_axis=dim, concat_axis=dim, tiled=True)
 
 
 def local(queries, latent_cache, lengths, value_weight, output_weight):
@@ -25,7 +31,7 @@
     swapped = lax.all_to_all(latent, "tp", split_axis=1, concat_axis=0, tiled=True)
     values = jnp.einsum("qhd,hde->qhe", swapped, value_weight, preferred_element_type=jnp.float32)
     values = values.astype(jnp.bfloat16).reshape(groups, requests, -1)
-    everyone = lax.all_gather(values, "dp", axis=1, tiled=True)
+    everyone = gather_from_all(values, "dp", 1)
     all_values = everyone.reshape(groups * columns * requests, -1)
     summed = lax.psum_scatter(
         jnp.dot(all_values, output_weight, preferred_element_type=jnp.float32),

time: 204 us -> 177 us (0.87)
  waiting for transfers between devices: 142 us -> 54.4 us
  blocking collectives: 37.2 us -> 99.7 us
    all_gather x1 -> x0, waiting for transfers between devices: 83.9 us -> none  [local(): everyone = lax.all_gather(values, 'dp', axis=1, tiled=True)]
    all_to_all x0 -> x1, blocking collectives: none -> 62.7 us  [gather_from_all(): lax.all_to_all(jnp.tile(x, repeats), axis, split_axis=dim, concat_axis=di...]
    reduce_scatter x1, waiting for transfers between devices: 57.8 us -> 54.3 us  [local(): lax.psum_scatter(jnp.dot(all_values, output_weight, preferred_element_typ...]
    all_gather x1 -> x0, local copies, waits for them, and re-layouts: 2.74 us -> none  [local(): everyone = lax.all_gather(values, 'dp', axis=1, tiled=True)]
  transfers between devices with their start and end apart: 2 -> 1, of which waited for: 2 -> 1; matrix products, arithmetic and copies ran while one was open for 0% -> 0% of each run, Pallas kernels for 0% -> 0%
where the time goes in v1:
time: 177 us
  blocking collectives  99.7 us (56%)
  waiting for transfers between devices  54.4 us (31%)
  between operations  13.5 us (8%)
  matrix products  5.14 us (3%)
  local copies, waits for them, and re-layouts  2.82 us (2%)
    all_to_all x1, blocking collectives, gather_from_all(): lax.all_to_all(jnp.tile(x, repeats), axis, split_axis=dim, concat_axis=di...  62.7 us
    reduce_scatter x1, waiting for transfers between devices, local(): lax.psum_scatter(jnp.dot(all_values, output_weight, preferred_element_typ...  54.3 us
    all_to_all x1, blocking collectives, local(): lax.all_to_all(rounded, 'dp', split_axis=0, concat_axis=1, tiled=True)  18.8 us
    all_to_all x1, blocking collectives, local(): lax.all_to_all(latent, 'tp', split_axis=1, concat_axis=0, tiled=True)  18.2 us
  transfers between devices with their start and end apart: 1, of which 1 were waited for; matrix products, arithmetic and copies ran while one was open for 0% of the time, Pallas kernels for 0%

profile of v1, /device:TPU:2, one launch (start us, length us, event | category | flops | bytes accessed | tf_op | source)
XLA Modules:
  0.0 176.5 jit_solution(12853668163846815299)
XLA Ops:
  6.5 0.0 copy-start
  6.5 0.0 reduce-scatter.2.cloned.1.call-start
  6.5 1.5 fusion.3
  8.1 0.2 fusion.8
  8.3 1.6 fusion.5
  9.9 0.3 copy.16
  10.2 18.2 %all_to_all.42 = bf16[2,128,512]{2,0,1:T(2,128)(2,1)S(1)} all-to-all(bf16[2,128,512]{2,0,1:T(2,128)(2,1)S(1)} %copy.16), channel_id=1, replica_groups=mesh['dp'=32,'tp'=16] {'tp'}, dimensions={1} | all-to-all | bytes 524288 | tf_op jit(solution)/shard_map/all_to_all | solution.py:31
  28.4 0.2 copy.23
  28.6 0.1 all_to_all.33
  28.7 0.0 copy-done
  28.7 0.3 fusion.4
  29.1 0.2 tile.11
  29.3 62.7 %all_to_all.43 = bf16[16,64,1024]{2,0,1:T(8,128)(2,1)S(1)} all-to-all(bf16[16,64,1024]{2,0,1:T(8,128)(2,1)S(1)} %bitcast.21), channel_id=1, replica_groups=mesh['dp'=32,'tp'=16] {'dp'}, dimensions={1} | all-to-all | bytes 4194304 | tf_op jit(solution)/shard_map/all_to_all | solution.py:12
  92.0 0.0 copy-start.1
  92.0 1.2 copy.20
  93.2 0.0 copy-done.1
  93.2 1.7 fusion.9
  94.9 0.0 reduce-scatter.2.cloned.1.call-update
  94.9 54.3 %reduce-scatter.2.cloned.1.call-done = f32[64,224]{1,0:T(8,128)} async-done(((f32[1024,224]{1,0:T(8,128)}), f32[64,224]{1,0:T(8,128)}) %reduce-scatter.2.cloned.1.call-update) | async-done | bytes 57360 | tf_op jit(solution)/shard_map/reduce_scatter | solution.py:36
  149.3 0.8 convert_element_type.16
  150.1 18.8 %all_to_all.44 = bf16[32,2,224]{2,1,0:T(2,128)(2,1)S(1)} all-to-all(bf16[32,2,224]{2,1,0:T(2,128)(2,1)S(1)} %all_to_all.35), channel_id=1, replica_groups=mesh['dp'=32,'tp'=16] {'dp'}, dimensions={0} | all-to-all | bytes 57344 | tf_op jit(solution)/shard_map/all_to_all | solution.py:43
  168.9 0.7 all_to_all.38
  (6 shorter events, 0.1 us)
Async XLA Ops:
  6.5 22.1 %copy-start = (bf16[8,512,128]{2,1,0:T(8,128)(2,1)S(1)}, bf16[8,512,128]{2,1,0:T(8,128)(2,1)}, u32[]{:S(2)}) copy-start(bf16[8,512,128]{2,1,0:T(8,128)(2,1)} %param.8) | copy-start | bytes 3145732
  6.5 142.7 %reduce-scatter.2.cloned.1.call-start = ((), (), s32[]{:S(2)}) async-start(), calls=%async_computation.4 | async-start | bytes 1114112 | tf_op jit(solution)/shard_map/reduce_scatter | solution.py:36
  92.0 1.2 copy-start.1
Sparse Core Ops, SparseCore 0:
  95.0 54.1 reduce-scatter.1
